TPU v7x, 32 devices: a whole 2x2x4 slice. The times are simulated.
32 devices in a mesh: dp: 4 (over y, x), segment: 2 (over core), band: 4 (over z).
Axes of the slice: x: 2, y: 2, z: 4, core: 2. Of those that a mesh axis runs over, the one named last changes fastest.
Arguments:
- fields: bfloat16 [4, 2, 32, 16, 512], P('dp', None, 'band'), may hold values from -6 to 6
- cell_mask: int32 [4, 2, 32, 16], P('dp', None, 'band'), may hold values 0 or 1
- merge_weight: bfloat16 [2, 1024, 512], P('segment', 'dp'), may hold values from -0.1875 to 0.1875
- qkv_weight: bfloat16 [2, 512, 1536], P('segment', 'dp')
- out_weight: bfloat16 [2, 512, 512], P('segment', 'dp'), may hold values from -1 to 1
- norm_gain: bfloat16 [2, 512], P('segment', 'dp'), may hold values from 0.099609375 to 1.8984375
- out_cotangent: bfloat16 [4, 2, 32, 16, 512], P('dp', None, 'band'), may hold values from -6 to 6
Outputs:
- section_out: bfloat16 [2, 4, 2, 32, 16, 512], P('segment', 'dp', None, 'band')
- merge_grad: float32 [2, 1024, 512], P('segment', 'dp')
- qkv_grad: float32 [2, 512, 1536], P('segment', 'dp')
- out_grad: float32 [2, 512, 512], P('segment', 'dp')
- gain_grad: float32 [2, 512], P('segment', 'dp')
Inputs may be any that keep to these rules, and one draw needn't show every extreme that they name: `cell_mask`: 1 marks a cell whose keys may be attended.
All inputs are finite; a program needn't handle non-finite values. No bound on the sum of `cell_mask` on one device may be relied on, other than what follows from the above.
Results may differ from a plain program's by a relative error of at most 0.03.
Values may be sent and summed in bfloat16 or wider, within the bound.
No kernel may reach another device: no remote copies, remote signals or barrier semaphores. Data moves between devices by JAX's collectives and lax.ppermute only.
A program may use at most 128 MiB of HBM per device.

v0:
```python
import jax
import jax.numpy as jnp
from jax import lax
from jax.sharding import PartitionSpec as P

HEADS = 8
WH = 8
WW = 16
SH = 4
SW = 8
EPSILON = 1e-05
MASKED = -1e30


def padded(shard, sides, width):
    for axis, dim in sides:
        size, length = (lax.axis_size(axis), shard.shape[dim])
        up = [(i, (i + 1) % size) for i in range(size - 1)]
        down = [(j, i) for i, j in up]
        last = lax.slice_in_dim(shard, length - width, length, axis=dim)
        first = lax.slice_in_dim(shard, 0, width, axis=dim)
        before = lax.ppermute(last, axis, up)
        after = lax.ppermute(first, axis, down)
        shard = jnp.concatenate([before, shard, after], axis=dim)
    return shard


def normalize(update):
    average = jnp.mean(update, axis=-1, keepdims=True)
    centered = update - average
    spread = jnp.mean(centered * centered, axis=-1, keepdims=True)
    inverse = lax.rsqrt(spread + EPSILON)
    return (centered * inverse, inverse)


def window_pattern(lon_count):
    query_index = jnp.arange(WH * lon_count, dtype=jnp.int32)
    key_index = jnp.arange(2 * WH * lon_count, dtype=jnp.int32)
    query_row = query_index // lon_count
    query_col = query_index % lon_count
    key_row = key_index // lon_count
    key_col = key_index % lon_count
    lat_same = ((query_row + SH) // WH)[:, None] == (key_row // WH)[None, :]
    lon_same = ((query_col + SW) // WW)[:, None] == ((key_col + SW) // WW)[None, :]
    self_key = ((query_row + SH)[:, None] == key_row[None, :]) & (
        query_col[:, None] == key_col[None, :]
    )
    return (lat_same & lon_same, self_key)


def attend(queries, keyvals, usable):
    row_count, lon_count, feature = queries.shape
    blocks = row_count // WH
    head_dim = feature // HEADS
    query_blocks = queries.reshape(blocks, WH * lon_count, HEADS, head_dim)
    kv_blocks = keyvals.reshape(blocks + 1, WH * lon_count, 2, HEADS, head_dim)
    key_pairs = jnp.concatenate([kv_blocks[:-1], kv_blocks[1:]], axis=1)
    use_blocks = usable.reshape(blocks + 1, WH * lon_count)
    use_pairs = jnp.concatenate([use_blocks[:-1], use_blocks[1:]], axis=1)
    inside, self_key = window_pattern(lon_count)
    allowed = inside[None] & (use_pairs[:, None, :] | self_key[None])
    scores = jnp.einsum(
        "nqhd,nkhd->nhqk", query_blocks, key_pairs[:, :, 0], preferred_element_type=jnp.float32
    ) * head_dim ** (-0.5)
    scores = jnp.where(allowed[:, None], scores, MASKED)
    highest = jnp.max(scores, axis=-1, keepdims=True)
    weights = jnp.exp(scores - highest)
    attn_prob = (weights / jnp.sum(weights, axis=-1, keepdims=True)).astype(jnp.bfloat16)
    mixture = jnp.einsum(
        "nhqk,nkhd->nqhd", attn_prob, key_pairs[:, :, 1], preferred_element_type=jnp.float32
    )
    return mixture.reshape(row_count, lon_count, feature).astype(jnp.bfloat16)


def guarded(active, function, operands):

    def skipped(values):
        return jax.tree.map(jnp.zeros_like, function(values))

    return lax.cond(active, function, skipped, operands)


def project(joined, merge_full, qkv_full, gain_full):
    update = jnp.einsum("rwj,jd->rwd", joined, merge_full, preferred_element_type=jnp.float32)
    normed, inverse = normalize(update)
    hidden = (normed * gain_full.astype(jnp.float32)).astype(jnp.bfloat16)
    projected = jnp.einsum("rwd,de->rwe", hidden, qkv_full, preferred_element_type=jnp.float32)
    feature = update.shape[-1]
    queries = projected[..., :feature].astype(jnp.bfloat16)
    keyvals = projected[..., feature:].astype(jnp.bfloat16)
    return (update, normed, inverse, hidden, queries, keyvals)


def section_forward(active, joined, usable, merge_full, qkv_full, gain_full, out_full):
    update, normed, inverse, hidden, queries, own_keys = guarded(
        active, lambda rows_own: project(rows_own, merge_full, qkv_full, gain_full), joined
    )
    keyvals = padded(own_keys, (("band", 0),), SH)

    def finish(operands):
        update_in, query_in, keyval_in, usable_in = operands
        mixture = attend(query_in, keyval_in, usable_in)
        result = (
            update_in
            + jnp.einsum("rwd,de->rwe", mixture, out_full, preferred_element_type=jnp.float32)
        ).astype(jnp.bfloat16)
        return (mixture, result)

    mixture, result = guarded(active, finish, (update, queries, keyvals, usable))
    return (result, (joined, normed, inverse, hidden, queries, keyvals, mixture))


def attend_back(out_full, operands):
    grad_out, queries, keyvals, mixture, usable = operands
    grad_mixture = jnp.einsum(
        "rwe,de->rwd", grad_out, out_full, preferred_element_type=jnp.float32
    ).astype(jnp.bfloat16)
    unused, pull_back = jax.vjp(
        lambda query_in, keyval_in: attend(query_in, keyval_in, usable), queries, keyvals
    )
    grad_query, grad_keyval = pull_back(grad_mixture)
    grad_outw = jnp.einsum("rwd,rwe->de", mixture, grad_out, preferred_element_type=jnp.float32)
    return (grad_query, grad_keyval, grad_outw)


def fold_rims(grad_keyval, row_count):
    rim_rows = jnp.concatenate([grad_keyval[:SH], grad_keyval[SH + row_count :]], axis=0)
    returned = padded(rim_rows, (("band", 0),), SH)
    own_part = grad_keyval[SH : SH + row_count].astype(jnp.float32)
    return jnp.concatenate(
        [
            own_part[:SH] + returned[:SH].astype(jnp.float32),
            own_part[SH : row_count - SH],
            own_part[row_count - SH :] + returned[3 * SH :].astype(jnp.float32),
        ],
        axis=0,
    ).astype(jnp.bfloat16)


def back_core(qkv_full, gain_full, grad_query, grad_keyown, grad_out, normed, inverse):
    grad_proj = jnp.concatenate([grad_query, grad_keyown], axis=-1)
    grad_hidden = jnp.einsum("rwe,de->rwd", grad_proj, qkv_full, preferred_element_type=jnp.float32)
    grad_normed = grad_hidden * gain_full.astype(jnp.float32)
    grad_update = (
        grad_out.astype(jnp.float32)
        + inverse
        * (
            grad_normed
            - jnp.mean(grad_normed, axis=-1, keepdims=True)
            - normed * jnp.mean(grad_normed * normed, axis=-1, keepdims=True)
        )
    ).astype(jnp.bfloat16)
    return (grad_proj, grad_hidden, grad_update)


def body(fields, cell_mask, merge_weight, qkv_weight, out_weight, norm_gain, out_cotangent):
    merge_rows, qkv_rows, out_rows, gain_rows = (
        lax.all_gather(merge_weight, "dp", axis=1, tiled=True),
        lax.all_gather(qkv_weight, "dp", axis=1, tiled=True),
        lax.all_gather(out_weight, "dp", axis=1, tiled=True),
        lax.all_gather(norm_gain, "dp", axis=1, tiled=True),
    )
    merge_full = merge_rows[0]
    qkv_full = qkv_rows[0]
    inputs = fields[0]
    cotangent = out_cotangent[0]
    micro_count, row_count, lon_count, feature = inputs.shape
    mask_ext = padded(cell_mask[0], (("band", 1),), SH)
    usable_ext = mask_ext == 1
    section_count = lax.axis_size("segment")
    half_count = section_count // 2
    section_rank = lax.axis_index("segment")
    merge_all, qkv_all, out_all, gain_all = (
        lax.all_gather(merge_rows, "segment", axis=0, tiled=True),
        lax.all_gather(qkv_rows, "segment", axis=0, tiled=True),
        lax.all_gather(out_rows, "segment", axis=0, tiled=True),
        lax.all_gather(gain_rows, "segment", axis=0, tiled=True),
    )
    local_count = micro_count // section_count
    always = jnp.array(True)
    shipped = [[] for index in range(section_count)]
    pick = section_rank * local_count + 0
    inputs_now = lax.dynamic_index_in_dim(inputs, pick, 0, keepdims=False)
    cotangent_now = lax.dynamic_index_in_dim(cotangent, pick, 0, keepdims=False)
    usable_now = lax.dynamic_index_in_dim(usable_ext, pick, 0, keepdims=False)
    outputs = []
    records = []
    for index in range(section_count):
        chain_in = inputs_now if index == 0 else outputs[index - 1]
        side_in = inputs_now if index < half_count else outputs[section_count - 1 - index]
        joined = jnp.concatenate([chain_in, side_in], axis=-1)
        result, record = section_forward(
            always,
            joined,
            usable_now,
            merge_all[index],
            qkv_all[index],
            gain_all[index],
            out_all[index],
        )
        outputs.append(result)
        records.append(record)
    flows = [None] * section_count
    for index in range(section_count - 1, -1, -1):
        grad_out = (
            cotangent_now if index == section_count - 1 else flows[index].astype(jnp.bfloat16)
        )
        joined, normed, inverse, hidden, queries, keyvals, mixture = records[index]
        grad_query, grad_keyval, unused = attend_back(
            out_all[index], (grad_out, queries, keyvals, mixture, usable_now)
        )
        grad_keyown = fold_rims(grad_keyval, row_count)
        grad_proj, unused, grad_update = back_core(
            qkv_all[index], gain_all[index], grad_query, grad_keyown, grad_out, normed, inverse
        )
        grad_joined = jnp.einsum(
            "rwd,jd->rwj", grad_update, merge_all[index], preferred_element_type=jnp.float32
        )
        grad_chain = grad_joined[..., :feature].astype(jnp.bfloat16).astype(jnp.float32)
        grad_side = grad_joined[..., feature:].astype(jnp.bfloat16).astype(jnp.float32)
        if index > 0:
            flows[index - 1] = grad_chain
        if index >= half_count:
            target = section_count - 1 - index
            flows[target] = flows[target] + grad_side
        shipped[index].append(
            (outputs[index], joined, grad_update, hidden, grad_proj, mixture, grad_out)
        )
    packed = tuple(
        (
            jnp.stack([jnp.stack([shipped[index][0][field]]) for index in range(section_count)])
            for field in range(7)
        )
    )
    home = (
        lax.all_to_all(packed[0], "segment", split_axis=0, concat_axis=1, tiled=True),
        lax.all_to_all(packed[1], "segment", split_axis=0, concat_axis=1, tiled=True),
        lax.all_to_all(packed[2], "segment", split_axis=0, concat_axis=1, tiled=True),
        lax.all_to_all(packed[3], "segment", split_axis=0, concat_axis=1, tiled=True),
        lax.all_to_all(packed[4], "segment", split_axis=0, concat_axis=1, tiled=True),
        lax.all_to_all(packed[5], "segment", split_axis=0, concat_axis=1, tiled=True),
        lax.all_to_all(packed[6], "segment", split_axis=0, concat_axis=1, tiled=True),
    )
    joined_all, grad_update_all, hidden_all, grad_proj_all, mixture_all, grad_out_all = [
        part[0] for part in home[1:]
    ]
    grad_merge = jnp.einsum(
        "mrwj,mrwd->jd", joined_all, grad_update_all, preferred_element_type=jnp.float32
    )
    grad_qkv = jnp.einsum(
        "mrwd,mrwe->de", hidden_all, grad_proj_all, preferred_element_type=jnp.float32
    )
    grad_outw = jnp.einsum(
        "mrwd,mrwe->de", mixture_all, grad_out_all, preferred_element_type=jnp.float32
    )
    update_all = jnp.einsum(
        "mrwj,jd->mrwd", joined_all, merge_full, preferred_element_type=jnp.float32
    )
    normed_all, unused = normalize(update_all)
    grad_hidden_all = jnp.einsum(
        "mrwe,de->mrwd", grad_proj_all, qkv_full, preferred_element_type=jnp.float32
    )
    grad_gain = jnp.sum(grad_hidden_all * normed_all, axis=(0, 1, 2))
    grad_sums = (grad_merge, grad_qkv, grad_outw, grad_gain)
    section_home = home[0][None]
    merge_part_sum, qkv_part_sum, out_part_sum, gain_part_sum = (
        lax.psum_scatter(
            grad_sums[0][None].astype(jnp.bfloat16), "dp", scatter_dimension=1, tiled=True
        ).astype(jnp.float32),
        lax.psum_scatter(
            grad_sums[1][None].astype(jnp.bfloat16), "dp", scatter_dimension=1, tiled=True
        ).astype(jnp.float32),
        lax.psum_scatter(
            grad_sums[2][None].astype(jnp.bfloat16), "dp", scatter_dimension=1, tiled=True
        ).astype(jnp.float32),
        lax.psum_scatter(
            grad_sums[3][None].astype(jnp.bfloat16), "dp", scatter_dimension=1, tiled=True
        ).astype(jnp.float32),
    )
    merge_grad, qkv_grad, out_grad, gain_grad = (
        lax.psum(merge_part_sum.astype(jnp.bfloat16), "band").astype(jnp.float32),
        lax.psum(qkv_part_sum.astype(jnp.bfloat16), "band").astype(jnp.float32),
        lax.psum(out_part_sum.astype(jnp.bfloat16), "band").astype(jnp.float32),
        lax.psum(gain_part_sum.astype(jnp.bfloat16), "band").astype(jnp.float32),
    )
    return (section_home, merge_grad, qkv_grad, out_grad, gain_grad)


def solution(mesh):
    return jax.shard_map(
        body,
        mesh=mesh,
        in_specs=(
            P("dp", None, "band", None, None),
            P("dp", None, "band", None),
            P("segment", "dp", None),
            P("segment", "dp", None),
            P("segment", "dp", None),
            P("segment", "dp"),
            P("dp", None, "band", None, None),
        ),
        out_specs=(
            P("segment", "dp", None, "band", None, None),
            P("segment", "dp", None),
            P("segment", "dp", None),
            P("segment", "dp", None),
            P("segment", "dp"),
        ),
        check_vma=False,
    )
```

profile of v0, /device:TPU:0, one launch (start us, length us, event | category | flops | bytes accessed | tf_op | source)
XLA Modules:
  0.0 377.2 jit_solution(2174182986141230632)
XLA Ops:
  8.8 30.4 %all-gather.7.cloned.1.call-done = bf16[1,1024,512]{2,1,0:T(8,128)(2,1)} async-done(((bf16[1,256,512]{2,1,0:T(8,128)(2,1)}), bf16[1,1024,512]{2,1,0:T(8,128)(2,1)}) %all-gather.7.cloned.1.call-update) | async-done | bytes 1048592 | tf_op jit(solution)/shard_map/all_gather | solution.py:158
  39.2 32.6 %all-gather.11.cloned.1.call-done = bf16[1,512,1536]{2,1,0:T(8,128)(2,1)} async-done(((bf16[1,128,1536]{2,1,0:T(8,128)(2,1)}), bf16[1,512,1536]{2,1,0:T(8,128)(2,1)}) %all-gather.11.cloned.1.call-update) | async-done | bytes 1572880 | tf_op jit(solution)/shard_map/all_gather | solution.py:159
  71.9 1.3 collective-permute-start.3
  73.2 4.5 %collective-permute-start.2 = (s32[2,4,16]{2,1,0:T(4,128)S(1)}, s32[2,4,16]{2,1,0:T(4,128)S(1)}, u32[]{:S(2)}, u32[]{:S(2)}) collective-permute-start(s32[2,4,16]{2,1,0:T(4,128)S(1)} %get-tuple-element.47), channel_id=1, source_target_pairs={{0,1},{1,2},{2,3},{4,5},{5,6},{6,7},{8,9},{9,10},{10,11},{12,13},{... | collective-permute-start | bytes 1544 | tf_op jit(solution)/shard_map/ppermute | solution.py:22
  77.8 10.6 %all_gather.30 = bf16[1,512,512]{2,1,0:T(8,128)(2,1)} all-gather(bf16[1,128,512]{2,1,0:T(8,128)(2,1)S(1)} %copy-done.33), channel_id=1, replica_groups=mesh['dp'=4,'segment'=2,'band'=4] {'dp'}, dimensions={1}, use_global_device_ids=true | all-gather | bytes 655360 | tf_op jit(solution)/shard_map/all_gather | solution.py:160
  88.5 7.1 %all_gather.26 = bf16[1,512]{1,0:T(2,128)(2,1)S(1)} all-gather(bf16[1,128]{1,0:T(2,128)(2,1)S(1)} %copy-done.44), channel_id=1, replica_groups=mesh['dp'=4,'segment'=2,'band'=4] {'dp'}, dimensions={1}, use_global_device_ids=true | all-gather | bytes 1280 | tf_op jit(solution)/shard_map/all_gather | solution.py:161
  95.6 1.8 all-gather
  98.5 1.6 fusion.133
  100.4 1.8 convolution_convert_fusion.1
  102.3 3.4 collective-permute-start
  105.7 1.3 collective-permute-start.1
  107.0 3.3 all-gather.15.cloned.1.call-done
  110.3 1.3 convolution_convert_fusion.10
  117.3 1.4 fusion.23
  118.7 1.6 fusion.135
  120.6 1.1 convolution_convert_fusion
  123.8 1.1 reshape.683
  125.8 3.4 collective-permute-start.4
  129.2 1.5 collective-permute-start.5
  131.2 1.4 collective-permute-done.4
  132.7 3.8 %collective-permute-done.5 = bf16[4,16,1024]{2,1,0:T(8,128)(2,1)S(1)} collective-permute-done((bf16[4,16,1024]{2,1,0:T(8,128)(2,1)S(1)}, bf16[4,16,1024]{2,1,0:T(8,128)(2,1)S(1)}, u32[]{:S(2)}, u32[]{:S(2)}) %collective-permute-start.5) | collective-permute-done | bytes 131104 | tf_op jit(solution)/shard_map/ppermute | solution.py:23
  136.5 1.7 pad_maximum_fusion.4
  139.0 1.3 slice.202
  140.8 1.3 fusion.136
  143.2 1.0 fusion.124
  144.3 1.7 fusion.19
  146.0 1.6 fusion.28
  149.3 4.1 %all-to-all-start.5 = ((bf16[2,1,8,16,512]{4,3,2,1,0:T(8,128)(2,1)}), bf16[2,1,8,16,512]{4,3,2,1,0:T(8,128)(2,1)}, u32[]{:S(2)}, u32[]{:S(2)}) async-start(bf16[2,1,8,16,512]{4,3,2,1,0:T(8,128)(2,1)} %pad_maximum_fusion.13), calls=%async_computation.7 | async-start | bytes 524288 | tf_op jit(solution)/shard_map/all_to_all | solution.py:241
  153.5 1.1 copy.60
  154.8 1.1 fusion.64
  156.7 1.8 copy.63
  158.5 1.5 reshape.688
  160.0 1.0 fusion.128
  161.1 3.4 collective-permute-start.6
  164.4 1.5 collective-permute-start.7
  166.0 1.0 slice_convert_fusion.1
  167.8 4.1 %collective-permute-done.7 = bf16[4,16,1024]{2,1,0:T(8,128)(2,1)S(1)} collective-permute-done((bf16[4,16,1024]{2,1,0:T(8,128)(2,1)S(1)}, bf16[4,16,1024]{2,1,0:T(8,128)(2,1)S(1)}, u32[]{:S(2)}, u32[]{:S(2)}) %collective-permute-start.7) | collective-permute-done | bytes 131104 | tf_op jit(solution)/shard_map/ppermute | solution.py:23
  172.0 2.3 fusion.126
  178.3 1.7 fusion.29
  180.0 1.0 fusion.20
  183.2 3.4 collective-permute-start.8
  186.6 1.3 collective-permute-start.9
  187.9 1.1 collective-permute-done.8
  189.1 4.4 %collective-permute-done.9 = bf16[4,16,1024]{2,1,0:T(8,128)(2,1)S(1)} collective-permute-done((bf16[4,16,1024]{2,1,0:T(8,128)(2,1)S(1)}, bf16[4,16,1024]{2,1,0:T(8,128)(2,1)S(1)}, u32[]{:S(2)}, u32[]{:S(2)}) %collective-permute-start.9) | collective-permute-done | bytes 131104 | tf_op jit(solution)/shard_map/ppermute | solution.py:23
  193.5 2.2 fusion.125
  196.0 3.9 %all_to_all.28 = bf16[2,1,8,16,512]{4,3,2,1,0:T(8,128)(2,1)S(1)} all-to-all(bf16[2,1,8,16,512]{4,3,2,1,0:T(8,128)(2,1)S(1)} %pad_maximum_fusion.14), channel_id=1, replica_groups=mesh['dp'=4,'segment'=2,'band'=4] {'segment'}, dimensions={0} | all-to-all | bytes 524288 | tf_op jit(solution)/shard_map/all_to_all | solution.py:242
  199.9 2.1 fusion.10
  203.0 3.5 all-to-all-start.1
  206.5 1.6 all-to-all-done.1
  208.2 3.9 %all_to_all.29 = bf16[2,1,8,16,512]{4,3,2,1,0:T(8,128)(2,1)S(1)} all-to-all(bf16[2,1,8,16,512]{4,3,2,1,0:T(8,128)(2,1)S(1)} %pad_maximum_fusion.11), channel_id=1, replica_groups=mesh['dp'=4,'segment'=2,'band'=4] {'segment'}, dimensions={0} | all-to-all | bytes 524288 | tf_op jit(solution)/shard_map/all_to_all | solution.py:238
  212.1 1.5 fusion.6
  214.4 3.4 all-to-all-start.3
  218.0 1.4 all-to-all-done.3
  220.1 4.4 %all_to_all.30 = bf16[2,1,8,16,1536]{4,3,2,1,0:T(8,128)(2,1)S(1)} all-to-all(bf16[2,1,8,16,1536]{4,3,2,1,0:T(8,128)(2,1)S(1)} %pad_maximum_fusion), channel_id=1, replica_groups=mesh['dp'=4,'segment'=2,'band'=4] {'segment'}, dimensions={0} | all-to-all | bytes 1572864 | tf_op jit(solution)/shard_map/all_to_all | solution.py:240
  224.4 2.8 fusion.1
  230.3 26.1 %reduce-scatter.7.cloned.1.call-done = bf16[1,256,512]{2,1,0:T(8,128)(2,1)} async-done(((bf16[1,1024,512]{2,1,0:T(8,128)(2,1)}), bf16[1,256,512]{2,1,0:T(8,128)(2,1)}) %reduce-scatter.7.cloned.1.call-update) | async-done | bytes 262160 | tf_op jit(solution)/shard_map/reduce_scatter | solution.py:267
  256.3 34.2 %reduce-scatter.9.cloned.1.call-done = bf16[1,128,1536]{2,1,0:T(8,128)(2,1)} async-done(((bf16[1,512,1536]{2,1,0:T(8,128)(2,1)}), bf16[1,128,1536]{2,1,0:T(8,128)(2,1)}) %reduce-scatter.9.cloned.1.call-update) | async-done | bytes 393232 | tf_op jit(solution)/shard_map/reduce_scatter | solution.py:270
  291.0 3.9 %all_to_all.31 = bf16[2,1,8,16,512]{4,3,2,1,0:T(8,128)(2,1)S(1)} all-to-all(bf16[2,1,8,16,512]{4,3,2,1,0:T(8,128)(2,1)S(1)} %pad_maximum_fusion.10), channel_id=1, replica_groups=mesh['dp'=4,'segment'=2,'band'=4] {'segment'}, dimensions={0} | all-to-all | bytes 524288 | tf_op jit(solution)/shard_map/all_to_all | solution.py:236
  295.0 23.0 %reduce-scatter.13.cloned.1.call-done = bf16[128,1]{1,0:T(8,128)(2,1)} async-done(((bf16[512,1]{1,0:T(8,128)(2,1)}), bf16[128,1]{1,0:T(8,128)(2,1)}) %reduce-scatter.13.cloned.1.call-update) | async-done | bytes 272
  318.8 11.7 %psum.31 = bf16[1,128]{1,0:T(2,128)(2,1)S(1)} all-reduce(bf16[1,128]{1,0:T(2,128)(2,1)S(1)} %copy.77), channel_id=1, replica_groups=mesh['dp'=4,'segment'=2,'band'=4] {'band'}, use_global_device_ids=true, to_apply=%region_28.29 | all-reduce | flops 128 | bytes 512 | tf_op jit(solution)/shard_map/psum | solution.py:284
  331.0 33.2 %all-reduce.11.cloned.1.call-done = (bf16[1,256,512]{2,1,0:T(8,128)(2,1)}, bf16[1,128,1536]{2,1,0:T(8,128)(2,1)}, bf16[1,128,512]{2,1,0:T(8,128)(2,1)}) async-done(((bf16[1,256,512]{2,1,0:T(8,128)(2,1)}, bf16[1,128,1536]{2,1,0:T(8,128)(2,1)}, bf16[1,128,512]{2,1,0:T(8,128)(2,1)}), (bf16[1,256,512]{2,1,0:T(8,128)(2,1)}, bf16[1,128,1536]{2,1,0:T(8,128)(2,1)}, ...) | async-done | bytes 786448 | tf_op jit(solution)/shard_map/psum | solution.py:281
  364.3 1.8 convert_element_type.336
  366.1 1.6 convert_element_type.344
  367.7 2.0 convert_element_type.339
  (228 shorter events, 32.4 us)
Async XLA Ops:
  7.2 90.8 %copy-start = (bf16[1,2,8,16,512]{4,3,2,1,0:T(8,128)(2,1)S(1)}, bf16[1,2,8,16,512]{4,3,2,1,0:T(8,128)(2,1)}, u32[]{:S(2)}) copy-start(bf16[1,2,8,16,512]{4,3,2,1,0:T(8,128)(2,1)} %param.7) | copy-start | bytes 786436
  7.2 64.7 %copy-start.35 = (s32[1,2,8,16]{3,2,1,0:T(8,128)S(1)}, s32[1,2,8,16]{3,2,1,0:T(8,128)}, u32[]{:S(2)}) copy-start(s32[1,2,8,16]{3,2,1,0:T(8,128)} %param.8) | copy-start | bytes 3076
  7.2 70.6 %copy-start.33 = (bf16[1,128,512]{2,1,0:T(8,128)(2,1)S(1)}, bf16[1,128,512]{2,1,0:T(8,128)(2,1)}, u32[]{:S(2)}) copy-start(bf16[1,128,512]{2,1,0:T(8,128)(2,1)} %param.11) | copy-start | bytes 393220
  7.2 31.9 %all-gather.7.cloned.1.call-start = ((), (), s32[]{:S(2)}) async-start(), calls=%async_computation.11 | async-start | bytes 1310720 | tf_op jit(solution)/shard_map/all_gather | solution.py:158
  7.9 80.5 %copy-start.44 = (bf16[1,128]{1,0:T(2,128)(2,1)S(1)}, bf16[1,128]{1,0:T(2,128)(2,1)}, u32[]{:S(2)}) copy-start(bf16[1,128]{1,0:T(2,128)(2,1)} %param.12) | copy-start | bytes 772
  7.9 63.9 %all-gather.11.cloned.1.call-start = ((), (), s32[]{:S(2)}) async-start(), calls=%async_computation.13 | async-start | bytes 1966080 | tf_op jit(solution)/shard_map/all_gather | solution.py:159
  8.7 89.3 %copy-start.28 = (bf16[1,2,8,16,512]{4,3,2,1,0:T(8,128)(2,1)S(1)}, bf16[1,2,8,16,512]{4,3,2,1,0:T(8,128)(2,1)}, u32[]{:S(2)}) copy-start(bf16[1,2,8,16,512]{4,3,2,1,0:T(8,128)(2,1)} %param.13) | copy-start | bytes 786436
  8.7 89.8 %all-gather.9.cloned.1.call-start = ((), (), s32[]{:S(2)}) async-start(), calls=%async_computation.12 | async-start | bytes 3145728 | tf_op jit(solution)/shard_map/all_gather | solution.py:174
  39.1 61.2 %all-gather.13.cloned.1.call-start = ((), (), s32[]{:S(2)}) async-start(), calls=%async_computation.14 | async-start | bytes 4718592 | tf_op jit(solution)/shard_map/all_gather | solution.py:175
  71.8 38.5 %all-gather.15.cloned.1.call-start = ((), (), s32[]{:S(2)}) async-start(), calls=%async_computation.15 | async-start | bytes 1572864 | tf_op jit(solution)/shard_map/all_gather | solution.py:176
  71.9 26.2 %collective-permute-start.3 = (s32[2,4,16]{2,1,0:T(4,128)S(1)}, s32[2,4,16]{2,1,0:T(4,128)S(1)}, u32[]{:S(2)}, u32[]{:S(2)}) collective-permute-start(s32[2,4,16]{2,1,0:T(4,128)S(1)} %get-tuple-element.46), channel_id=1, source_target_pairs={{1,0},{2,1},{3,2},{5,4},{6,5},{7,6},{9,8},{10,9},{11,10},{13,12},{... | collective-permute-start | bytes 1544 | tf_op jit(solution)/shard_map/ppermute | solution.py:23
  73.2 24.9 %collective-permute-start.2 = (s32[2,4,16]{2,1,0:T(4,128)S(1)}, s32[2,4,16]{2,1,0:T(4,128)S(1)}, u32[]{:S(2)}, u32[]{:S(2)}) collective-permute-start(s32[2,4,16]{2,1,0:T(4,128)S(1)} %get-tuple-element.47), channel_id=1, source_target_pairs={{0,1},{1,2},{2,3},{4,5},{5,6},{6,7},{8,9},{9,10},{10,11},{12,13},{... | collective-permute-start | bytes 1544 | tf_op jit(solution)/shard_map/ppermute | solution.py:22
  98.0 4.2 %copy-start.41 = (f32[1,1,512]{2,1,0:T(1,128)}, f32[1,1,512]{2,1,0:T(1,128)S(1)}, u32[]{:S(2)}) copy-start(f32[1,1,512]{2,1,0:T(1,128)S(1)} %get-tuple-element.49) | copy-start | bytes 6148
  98.0 4.2 %copy-start.13 = (bf16[8,16,512]{2,1,0:T(8,128)(2,1)}, bf16[8,16,512]{2,1,0:T(8,128)(2,1)S(1)}, u32[]{:S(2)}) copy-start(bf16[8,16,512]{2,1,0:T(8,128)(2,1)S(1)} %dynamic-slice_bitcast_fusion) | copy-start | bytes 393220
  98.0 12.3 %copy-start.16 = (bf16[1,1,8,16,512]{4,3,2,1,0:T(8,128)(2,1)}, bf16[1,1,8,16,512]{4,3,2,1,0:T(8,128)(2,1)S(1)}, u32[]{:S(2)}) copy-start(bf16[1,1,8,16,512]{4,3,2,1,0:T(8,128)(2,1)S(1)} %constant_dynamic-slice_fusion) | copy-start | bytes 393220
  98.5 16.0 %copy-start.25 = (pred[128,256]{1,0:T(8,128)(4,1)}, pred[128,256]{1,0:T(8,128)(4,1)S(1)}, u32[]{:S(2)}) copy-start(pred[128,256]{1,0:T(8,128)(4,1)S(1)} %or_and_fusion) | copy-start | bytes 98308
  100.1 17.2 %copy-start.6 = (f32[8,16,512]{2,1,0:T(8,128)}, f32[8,16,512]{2,1,0:T(8,128)S(1)}, u32[]{:S(2)}) copy-start(f32[8,16,512]{2,1,0:T(8,128)S(1)} %get-tuple-element.53) | copy-start | bytes 786436
  100.3 1.9 copy-start.36
  102.3 10.2 %collective-permute-start = (bf16[4,16,1024]{2,1,0:T(8,128)(2,1)S(1)}, bf16[4,16,1024]{2,1,0:T(8,128)(2,1)S(1)}, u32[]{:S(2)}, u32[]{:S(2)}) collective-permute-start(bf16[4,16,1024]{2,1,0:T(8,128)(2,1)S(1)} %get-tuple-element.35), channel_id=1, source_target_pairs={{0,1},{1,2},{2,3},{4,5},{5,6},{6,7},{8,9},{9,10},{10,11},{12,13},{... | collective-permute-start | bytes 393224 | tf_op jit(solution)/shard_map/ppermute | solution.py:22
  105.7 7.2 %collective-permute-start.1 = (bf16[4,16,1024]{2,1,0:T(8,128)(2,1)S(1)}, bf16[4,16,1024]{2,1,0:T(8,128)(2,1)S(1)}, u32[]{:S(2)}, u32[]{:S(2)}) collective-permute-start(bf16[4,16,1024]{2,1,0:T(8,128)(2,1)S(1)} %get-tuple-element.36), channel_id=1, source_target_pairs={{1,0},{2,1},{3,2},{5,4},{6,5},{7,6},{9,8},{10,9},{11,10},{13,12},{... | collective-permute-start | bytes 393224 | tf_op jit(solution)/shard_map/ppermute | solution.py:23
  112.5 2.0 copy-start.18
  117.3 3.3 copy-start.45
  118.7 3.0 copy-start.9
  120.4 4.5 %copy-start.4 = (f32[8,16,512]{2,1,0:T(8,128)}, f32[8,16,512]{2,1,0:T(8,128)S(1)}, u32[]{:S(2)}) copy-start(f32[8,16,512]{2,1,0:T(8,128)S(1)} %get-tuple-element.57) | copy-start | bytes 786436
  120.6 2.5 copy-start.38
  125.8 6.9 %collective-permute-start.4 = (bf16[4,16,1024]{2,1,0:T(8,128)(2,1)}, bf16[4,16,1024]{2,1,0:T(8,128)(2,1)S(1)}, u32[]{:S(2)}, u32[]{:S(2)}) collective-permute-start(bf16[4,16,1024]{2,1,0:T(8,128)(2,1)} %get-tuple-element.33), channel_id=1, source_target_pairs={{0,1},{1,2},{2,3},{4,5},{5,6},{6,7},{8,9},{9,10},{10,11},{12,13},{... | collective-permute-start | bytes 393224 | tf_op jit(solution)/shard_map/ppermute | solution.py:22
  129.2 7.3 %collective-permute-start.5 = (bf16[4,16,1024]{2,1,0:T(8,128)(2,1)S(1)}, bf16[4,16,1024]{2,1,0:T(8,128)(2,1)S(1)}, u32[]{:S(2)}, u32[]{:S(2)}) collective-permute-start(bf16[4,16,1024]{2,1,0:T(8,128)(2,1)S(1)} %get-tuple-element.34), channel_id=1, source_target_pairs={{1,0},{2,1},{3,2},{5,4},{6,5},{7,6},{9,8},{10,9},{11,10},{13,12},{... | collective-permute-start | bytes 393224 | tf_op jit(solution)/shard_map/ppermute | solution.py:23
  142.5 1.7 copy-start.20
  142.5 1.7 copy-start.26
  148.3 7.5 %copy-start.2 = (bf16[1,128,8,64]{3,2,1,0:T(8,128)(2,1)}, bf16[1,128,8,64]{3,2,1,0:T(8,128)(2,1)S(1)}, u32[]{:S(2)}) copy-start(bf16[1,128,8,64]{3,2,1,0:T(8,128)(2,1)S(1)} %copy.58) | copy-start | bytes 393220
  149.3 46.7 %all-to-all-start.5 = ((bf16[2,1,8,16,512]{4,3,2,1,0:T(8,128)(2,1)}), bf16[2,1,8,16,512]{4,3,2,1,0:T(8,128)(2,1)}, u32[]{:S(2)}, u32[]{:S(2)}) async-start(bf16[2,1,8,16,512]{4,3,2,1,0:T(8,128)(2,1)} %pad_maximum_fusion.13), calls=%async_computation.7 | async-start | bytes 524288 | tf_op jit(solution)/shard_map/all_to_all | solution.py:241
  153.4 76.8 %reduce-scatter.11.cloned.1.call-start = ((), (), s32[]{:S(2)}) async-start(), calls=%async_computation.18 | async-start | bytes 655360 | tf_op jit(solution)/shard_map/reduce_scatter | solution.py:273
  160.0 12.0 %copy-start.5 = (f32[8,16,512]{2,1,0:T(8,128)S(1)}, f32[8,16,512]{2,1,0:T(8,128)}, u32[]{:S(2)}) copy-start(f32[8,16,512]{2,1,0:T(8,128)} %copy-done.4) | copy-start | bytes 786436
  160.0 12.0 %copy-start.39 = (f32[8,16]{1,0:T(8,128)S(1)}, f32[8,16]{1,0:T(8,128)}, u32[]{:S(2)}) copy-start(f32[8,16]{1,0:T(8,128)} %copy-done.38) | copy-start | bytes 1540
  160.0 12.0 %copy-start.43 = (f32[1,1,512]{2,1,0:T(1,128)S(1)}, f32[1,1,512]{2,1,0:T(1,128)}, u32[]{:S(2)}) copy-start(f32[1,1,512]{2,1,0:T(1,128)} %get-tuple-element.48) | copy-start | bytes 6148
  161.1 6.7 %collective-permute-start.6 = (bf16[4,16,1024]{2,1,0:T(8,128)(2,1)S(1)}, bf16[4,16,1024]{2,1,0:T(8,128)(2,1)S(1)}, u32[]{:S(2)}, u32[]{:S(2)}) collective-permute-start(bf16[4,16,1024]{2,1,0:T(8,128)(2,1)S(1)} %get-tuple-element.29), channel_id=1, source_target_pairs={{0,1},{1,2},{2,3},{4,5},{5,6},{6,7},{8,9},{9,10},{10,11},{12,13},{... | collective-permute-start | bytes 393224 | tf_op jit(solution)/shard_map/ppermute | solution.py:22
  164.4 7.5 %collective-permute-start.7 = (bf16[4,16,1024]{2,1,0:T(8,128)(2,1)S(1)}, bf16[4,16,1024]{2,1,0:T(8,128)(2,1)S(1)}, u32[]{:S(2)}, u32[]{:S(2)}) collective-permute-start(bf16[4,16,1024]{2,1,0:T(8,128)(2,1)S(1)} %get-tuple-element.30), channel_id=1, source_target_pairs={{1,0},{2,1},{3,2},{5,4},{6,5},{7,6},{9,8},{10,9},{11,10},{13,12},{... | collective-permute-start | bytes 393224 | tf_op jit(solution)/shard_map/ppermute | solution.py:23
  167.0 7.4 %copy-start.29 = (bf16[1,2,8,16,512]{4,3,2,1,0:T(8,128)(2,1)S(1)}, bf16[1,2,8,16,512]{4,3,2,1,0:T(8,128)(2,1)}, u32[]{:S(2)}) copy-start(bf16[1,2,8,16,512]{4,3,2,1,0:T(8,128)(2,1)} %param.13) | copy-start | bytes 786436
  172.0 2.4 copy-start.21
  172.0 2.4 copy-start.23
  172.0 2.5 copy-start.46
  174.6 2.1 copy-start.40
  176.7 1.6 copy-start.27
  178.3 1.7 copy-start.19
  182.4 11.1 %copy-start.7 = (f32[8,16,512]{2,1,0:T(8,128)S(1)}, f32[8,16,512]{2,1,0:T(8,128)}, u32[]{:S(2)}) copy-start(f32[8,16,512]{2,1,0:T(8,128)} %copy-done.6) | copy-start | bytes 786436
  182.4 11.1 %copy-start.37 = (f32[8,16]{1,0:T(8,128)S(1)}, f32[8,16]{1,0:T(8,128)}, u32[]{:S(2)}) copy-start(f32[8,16]{1,0:T(8,128)} %copy-done.36) | copy-start | bytes 1540
  182.4 11.1 %copy-start.42 = (f32[1,1,512]{2,1,0:T(1,128)S(1)}, f32[1,1,512]{2,1,0:T(1,128)}, u32[]{:S(2)}) copy-start(f32[1,1,512]{2,1,0:T(1,128)} %copy-done.41) | copy-start | bytes 6148
  183.2 5.9 %collective-permute-start.8 = (bf16[4,16,1024]{2,1,0:T(8,128)(2,1)S(1)}, bf16[4,16,1024]{2,1,0:T(8,128)(2,1)S(1)}, u32[]{:S(2)}, u32[]{:S(2)}) collective-permute-start(bf16[4,16,1024]{2,1,0:T(8,128)(2,1)S(1)} %get-tuple-element.23), channel_id=1, source_target_pairs={{0,1},{1,2},{2,3},{4,5},{5,6},{6,7},{8,9},{9,10},{10,11},{12,13},{... | collective-permute-start | bytes 393224 | tf_op jit(solution)/shard_map/ppermute | solution.py:22
  186.6 6.9 %collective-permute-start.9 = (bf16[4,16,1024]{2,1,0:T(8,128)(2,1)S(1)}, bf16[4,16,1024]{2,1,0:T(8,128)(2,1)S(1)}, u32[]{:S(2)}, u32[]{:S(2)}) collective-permute-start(bf16[4,16,1024]{2,1,0:T(8,128)(2,1)S(1)} %get-tuple-element.24), channel_id=1, source_target_pairs={{1,0},{2,1},{3,2},{5,4},{6,5},{7,6},{9,8},{10,9},{11,10},{13,12},{... | collective-permute-start | bytes 393224 | tf_op jit(solution)/shard_map/ppermute | solution.py:23
  187.9 7.8 %copy-start.32 = (bf16[8,16,1024]{2,1,0:T(8,128)(2,1)S(1)}, bf16[8,16,1024]{2,1,0:T(8,128)(2,1)}, u32[]{:S(2)}) copy-start(bf16[8,16,1024]{2,1,0:T(8,128)(2,1)} %copy-done.31) | copy-start | bytes 786436
  193.5 2.4 copy-start.17
  199.9 2.1 copy-start.14
  199.9 2.2 copy-start.10
  203.0 5.2 %all-to-all-start.1 = ((bf16[2,1,8,16,1024]{4,3,2,1,0:T(8,128)(2,1)}), bf16[2,1,8,16,1024]{4,3,2,1,0:T(8,128)(2,1)S(1)}, u32[]{:S(2)}, u32[]{:S(2)}) async-start(bf16[2,1,8,16,1024]{4,3,2,1,0:T(8,128)(2,1)} %pad_maximum_fusion.1), calls=%async_computation.1 | async-start | bytes 1048576 | tf_op jit(solution)/shard_map/all_to_all | solution.py:237
  206.5 49.9 %reduce-scatter.7.cloned.1.call-start = ((), (), s32[]{:S(2)}) async-start(), calls=%async_computation.16 | async-start | bytes 1310720 | tf_op jit(solution)/shard_map/reduce_scatter | solution.py:267
  212.1 1.5 copy-start.22
  212.1 1.5 copy-start.24
  214.4 5.0 %all-to-all-start.3 = ((bf16[2,1,8,16,512]{4,3,2,1,0:T(8,128)(2,1)}), bf16[2,1,8,16,512]{4,3,2,1,0:T(8,128)(2,1)S(1)}, u32[]{:S(2)}, u32[]{:S(2)}) async-start(bf16[2,1,8,16,512]{4,3,2,1,0:T(8,128)(2,1)} %pad_maximum_fusion.12), calls=%async_computation.4 | async-start | bytes 524288 | tf_op jit(solution)/shard_map/all_to_all | solution.py:239
  217.8 72.7 %reduce-scatter.9.cloned.1.call-start = ((), (), s32[]{:S(2)}) async-start(), calls=%async_computation.17 | async-start | bytes 1966080 | tf_op jit(solution)/shard_map/reduce_scatter | solution.py:270
  224.4 2.9 copy-start.1
  227.3 90.7 %reduce-scatter.13.cloned.1.call-start = ((), (), s32[]{:S(2)}) async-start(), calls=%async_computation.19 | async-start | bytes 163840
  228.8 61.8 %copy-start.3 = (bf16[1,128,8,64]{3,2,1,0:T(8,128)(2,1)S(1)}, bf16[1,128,8,64]{3,2,1,0:T(8,128)(2,1)}, u32[]{:S(2)}) copy-start(bf16[1,128,8,64]{3,2,1,0:T(8,128)(2,1)} %copy-done.2) | copy-start | bytes 393220
  228.8 62.0 %copy-start.12 = (bf16[2,512,512]{2,1,0:T(8,128)(2,1)S(1)}, bf16[2,512,512]{2,1,0:T(8,128)(2,1)}, u32[]{:S(2)}) copy-start(bf16[2,512,512]{2,1,0:T(8,128)(2,1)} %all-gather.15.cloned.1.call-done) | copy-start | bytes 3145732
  230.2 134.1 %all-reduce.11.cloned.1.call-start = ((), (), s32[]{:S(2)}) async-start(), calls=%async_computation.20 | async-start | bytes 1572864 | tf_op jit(solution)/shard_map/psum | solution.py:281
  (6 other events, 6.2 us)
Sparse Core Ops, SparseCore 0:
  9.9 29.2 all-gather.6
  40.9 30.8 all-gather.10
  73.4 10.5 all-gather.8
  85.4 13.2 all-gather.12
  100.1 10.1 all-gather.14
  202.2 23.2 reduce-scatter.10
  228.3 27.9 reduce-scatter.6
  259.3 31.1 reduce-scatter.8
  293.8 24.1 reduce-scatter.12
  320.4 43.7 all-reduce.10
where the time goes:
time: 379 us; the launch traced here: 377 us
  waiting for transfers between devices  203 us (54%)
  blocking collectives  47.4 us (13%)
  starting transfers between devices  36.4 us (10%)
  matrix products  32 us (8%)
  local copies, waits for them, and re-layouts  23.7 us (6%)
  other arithmetic  18.8 us (5%)
  between operations  15.6 us (4%)
    reduce_scatter x1, waiting for transfers between devices, body(): lax.psum_scatter(grad_sums[1][None].astype(jnp.bfloat16), 'dp', scatter_d...  34.2 us
    psum x1, waiting for transfers between devices, body(): lax.psum(merge_part_sum.astype(jnp.bfloat16), 'band').astype(jnp.float32)  33.2 us
    all_gather x1, waiting for transfers between devices, body(): lax.all_gather(qkv_weight, 'dp', axis=1, tiled=True)  32.6 us
    all_gather x1, waiting for transfers between devices, body(): lax.all_gather(merge_weight, 'dp', axis=1, tiled=True)  30.4 us
    reduce_scatter x1, waiting for transfers between devices, body(): lax.psum_scatter(grad_sums[0][None].astype(jnp.bfloat16), 'dp', scatter_d...  26.1 us
    unnamed x11, waiting for transfers between devices  24.5 us
    ppermute x5, starting transfers between devices, padded(): before = lax.ppermute(last, axis, up)  18.1 us
    ppermute x5, waiting for transfers between devices, padded(): after = lax.ppermute(first, axis, down)  12.6 us
  transfers between devices with their start and end apart: 23, of which 16 were waited for; matrix products, arithmetic and copies ran while one was open for 10% of the time, Pallas kernels for 0%

commit v1 on v0

--- a/solution.py
+++ b/solution.py
@@ -278,7 +278,9 @@
         ).astype(jnp.float32),
     )
     merge_grad, qkv_grad, out_grad, gain_grad = (
-        lax.psum(merge_part_sum.astype(jnp.bfloat16), "band").astype(jnp.float32),
+        jnp.sum(lax.all_gather(merge_part_sum.astype(jnp.bfloat16), "band"), axis=0).astype(
+            jnp.float32
+        ),
         lax.psum(qkv_part_sum.astype(jnp.bfloat16), "band").astype(jnp.float32),
         lax.psum(out_part_sum.astype(jnp.bfloat16), "band").astype(jnp.float32),
         lax.psum(gain_part_sum.astype(jnp.bfloat16), "band").astype(jnp.float32),

time: 379 us -> 398 us (1.050)
  waiting for transfers between devices: 203 us -> 224 us
    reduce_scatter x1, waiting for transfers between devices: 26.1 us -> 0.02 us  [body(): lax.psum_scatter(grad_sums[0][None].astype(jnp.bfloat16), 'dp', scatter_d...]
    reduce_scatter x1, waiting for transfers between devices: 0.02 us -> 25.7 us  [body(): lax.psum_scatter(grad_sums[2][None].astype(jnp.bfloat16), 'dp', scatter_d...]
    all_gather x0 -> x1, waiting for transfers between devices: none -> 16.3 us  [body(): lax.all_gather(merge_part_sum.astype(jnp.bfloat16), 'band')]
    psum x1, waiting for transfers between devices: 33.2 us -> 38.2 us  [body(): lax.psum(qkv_part_sum.astype(jnp.bfloat16), 'band').astype(jnp.float32)]
    unnamed x11 -> x12, waiting for transfers between devices: 24.5 us -> 25.1 us
  transfers between devices with their start and end apart: 23 -> 24, of which waited for: 16 -> 16; matrix products, arithmetic and copies ran while one was open for 10% -> 14% of each run, Pallas kernels for 0% -> 0%
where the time goes in v1:
time: 398 us; the launch traced here: 396 us
  waiting for transfers between devices  224 us (56%)
  blocking collectives  47.5 us (12%)
  starting transfers between devices  35.9 us (9%)
  matrix products  33.5 us (8%)
  local copies, waits for them, and re-layouts  21.3 us (5%)
  other arithmetic  18.9 us (5%)
  between operations  15.4 us (4%)
    psum x1, waiting for transfers between devices, body(): lax.psum(qkv_part_sum.astype(jnp.bfloat16), 'band').astype(jnp.float32)  38.2 us
    reduce_scatter x1, waiting for transfers between devices, body(): lax.psum_scatter(grad_sums[1][None].astype(jnp.bfloat16), 'dp', scatter_d...  34.1 us
    all_gather x1, waiting for transfers between devices, body(): lax.all_gather(qkv_weight, 'dp', axis=1, tiled=True)  32.6 us
    all_gather x1, waiting for transfers between devices, body(): lax.all_gather(merge_weight, 'dp', axis=1, tiled=True)  30.4 us
    reduce_scatter x1, waiting for transfers between devices, body(): lax.psum_scatter(grad_sums[2][None].astype(jnp.bfloat16), 'dp', scatter_d...  25.7 us
    unnamed x12, waiting for transfers between devices  25.1 us
    ppermute x5, starting transfers between devices, padded(): before = lax.ppermute(last, axis, up)  17.5 us
    all_gather x1, waiting for transfers between devices, body(): lax.all_gather(merge_part_sum.astype(jnp.bfloat16), 'band')  16.3 us
  transfers between devices with their start and end apart: 24, of which 16 were waited for; matrix products, arithmetic and copies ran while one was open for 14% of the time, Pallas kernels for 0%

profile of v1, /device:TPU:0, one launch (start us, length us, event | category | flops | bytes accessed | tf_op | source)
XLA Modules:
  0.0 396.5 jit_solution(17636620124839370776)
XLA Ops:
  8.8 30.4 %all-gather.9.cloned.1.call-done = bf16[1,1024,512]{2,1,0:T(8,128)(2,1)} async-done(((bf16[1,256,512]{2,1,0:T(8,128)(2,1)}), bf16[1,1024,512]{2,1,0:T(8,128)(2,1)}) %all-gather.9.cloned.1.call-update) | async-done | bytes 1048592 | tf_op jit(solution)/shard_map/all_gather | solution.py:158
  39.2 32.6 %all-gather.13.cloned.1.call-done = bf16[1,512,1536]{2,1,0:T(8,128)(2,1)} async-done(((bf16[1,128,1536]{2,1,0:T(8,128)(2,1)}), bf16[1,512,1536]{2,1,0:T(8,128)(2,1)}) %all-gather.13.cloned.1.call-update) | async-done | bytes 1572880 | tf_op jit(solution)/shard_map/all_gather | solution.py:159
  71.9 1.3 collective-permute-start.3
  73.2 4.5 %collective-permute-start.2 = (s32[2,4,16]{2,1,0:T(4,128)S(1)}, s32[2,4,16]{2,1,0:T(4,128)S(1)}, u32[]{:S(2)}, u32[]{:S(2)}) collective-permute-start(s32[2,4,16]{2,1,0:T(4,128)S(1)} %get-tuple-element.46), channel_id=1, source_target_pairs={{0,1},{1,2},{2,3},{4,5},{5,6},{6,7},{8,9},{9,10},{10,11},{12,13},{... | collective-permute-start | bytes 1544 | tf_op jit(solution)/shard_map/ppermute | solution.py:22
  77.8 10.6 %all_gather.36 = bf16[1,512,512]{2,1,0:T(8,128)(2,1)} all-gather(bf16[1,128,512]{2,1,0:T(8,128)(2,1)S(1)} %copy-done.47), channel_id=1, replica_groups=mesh['dp'=4,'segment'=2,'band'=4] {'dp'}, dimensions={1}, use_global_device_ids=true | all-gather | bytes 655360 | tf_op jit(solution)/shard_map/all_gather | solution.py:160
  88.5 7.1 %all_gather.32 = bf16[1,512]{1,0:T(2,128)(2,1)S(1)} all-gather(bf16[1,128]{1,0:T(2,128)(2,1)S(1)} %copy-done.59), channel_id=1, replica_groups=mesh['dp'=4,'segment'=2,'band'=4] {'dp'}, dimensions={1}, use_global_device_ids=true | all-gather | bytes 1280 | tf_op jit(solution)/shard_map/all_gather | solution.py:161
  95.5 1.8 all-gather.1
  99.2 1.6 fusion.133
  101.0 1.8 convolution_convert_fusion.1
  102.9 3.4 collective-permute-start
  106.3 1.3 collective-permute-start.1
  107.6 2.7 all-gather.17.cloned.1.call-done
  110.3 1.3 convolution_convert_fusion.10
  112.5 0.9 collective-permute-done.1
  117.1 1.4 fusion.23
  118.6 1.6 fusion.135
  123.0 4.2 %all-to-all-start.1 = ((bf16[2,1,8,16,1024]{4,3,2,1,0:T(8,128)(2,1)}), bf16[2,1,8,16,1024]{4,3,2,1,0:T(8,128)(2,1)}, u32[]{:S(2)}, u32[]{:S(2)}) async-start(bf16[2,1,8,16,1024]{4,3,2,1,0:T(8,128)(2,1)} %pad_maximum_fusion.1), calls=%async_computation.1 | async-start | bytes 1048576 | tf_op jit(solution)/shard_map/all_to_all | solution.py:237
  127.7 3.4 collective-permute-start.4
  131.1 1.5 collective-permute-start.5
  133.2 1.6 collective-permute-done.4
  134.8 3.8 collective-permute-done.5
  141.8 1.0 fusion.124
  142.8 1.7 fusion.19
  144.5 1.7 fusion.28
  146.4 1.1 copy.60
  149.3 1.8 copy.63
  151.2 1.5 reshape.699
  152.7 1.0 fusion.128
  153.7 2.7 collective-permute-start.6
  156.5 1.5 collective-permute-start.7
  158.0 1.0 slice_convert_fusion.1
  159.0 4.3 %collective-permute-done.7 = bf16[4,16,1024]{2,1,0:T(8,128)(2,1)S(1)} collective-permute-done((bf16[4,16,1024]{2,1,0:T(8,128)(2,1)S(1)}, bf16[4,16,1024]{2,1,0:T(8,128)(2,1)S(1)}, u32[]{:S(2)}, u32[]{:S(2)}) %collective-permute-start.7) | collective-permute-done | bytes 131104 | tf_op jit(solution)/shard_map/ppermute | solution.py:23
  163.5 2.3 fusion.126
  169.1 1.1 copy.64
  172.7 1.7 fusion.29
  174.4 1.7 fusion.20
  177.1 1.1 fusion.65
  179.8 3.4 collective-permute-start.8
  183.2 1.3 collective-permute-start.9
  184.6 1.1 collective-permute-done.8
  185.7 4.4 %collective-permute-done.9 = bf16[4,16,1024]{2,1,0:T(8,128)(2,1)S(1)} collective-permute-done((bf16[4,16,1024]{2,1,0:T(8,128)(2,1)S(1)}, bf16[4,16,1024]{2,1,0:T(8,128)(2,1)S(1)}, u32[]{:S(2)}, u32[]{:S(2)}) %collective-permute-start.9) | collective-permute-done | bytes 131104 | tf_op jit(solution)/shard_map/ppermute | solution.py:23
  190.2 2.2 fusion.125
  192.7 3.9 all_to_all.28
  196.7 2.6 fusion.6
  201.0 3.4 all-to-all-start.5
  204.7 1.3 all-to-all-done.5
  206.0 3.9 all_to_all.29
  209.9 1.1 fusion.10
  211.8 3.4 all-to-all-start.3
  215.4 1.4 all-to-all-done.3
  216.8 4.4 %all_to_all.30 = bf16[2,1,8,16,1536]{4,3,2,1,0:T(8,128)(2,1)S(1)} all-to-all(bf16[2,1,8,16,1536]{4,3,2,1,0:T(8,128)(2,1)S(1)} %pad_maximum_fusion), channel_id=1, replica_groups=mesh['dp'=4,'segment'=2,'band'=4] {'segment'}, dimensions={0} | all-to-all | bytes 1572864 | tf_op jit(solution)/shard_map/all_to_all | solution.py:240
  221.1 1.8 fusion.1
  223.0 1.6 fusion.137
  224.8 2.1 fusion.14
  228.4 25.7 %reduce-scatter.11.cloned.1.call-done = bf16[1,128,512]{2,1,0:T(8,128)(2,1)} async-done(((bf16[1,512,512]{2,1,0:T(8,128)(2,1)}), bf16[1,128,512]{2,1,0:T(8,128)(2,1)}) %reduce-scatter.11.cloned.1.call-update) | async-done | bytes 131088 | tf_op jit(solution)/shard_map/reduce_scatter | solution.py:273
  254.1 34.1 %reduce-scatter.9.cloned.1.call-done = bf16[1,128,1536]{2,1,0:T(8,128)(2,1)} async-done(((bf16[1,512,1536]{2,1,0:T(8,128)(2,1)}), bf16[1,128,1536]{2,1,0:T(8,128)(2,1)}) %reduce-scatter.9.cloned.1.call-update) | async-done | bytes 393232 | tf_op jit(solution)/shard_map/reduce_scatter | solution.py:270
  288.7 3.9 all_to_all.31
  292.7 23.1 %reduce-scatter.13.cloned.1.call-done = bf16[128,1]{1,0:T(8,128)(2,1)} async-done(((bf16[512,1]{1,0:T(8,128)(2,1)}), bf16[128,1]{1,0:T(8,128)(2,1)}) %reduce-scatter.13.cloned.1.call-update) | async-done | bytes 272
  316.6 11.8 %psum.23 = bf16[1,128]{1,0:T(2,128)(2,1)S(1)} all-reduce(bf16[1,128]{1,0:T(2,128)(2,1)S(1)} %copy.77), channel_id=1, replica_groups=mesh['dp'=4,'segment'=2,'band'=4] {'band'}, use_global_device_ids=true, to_apply=%region_28.29 | all-reduce | flops 128 | bytes 512 | tf_op jit(solution)/shard_map/psum | solution.py:286
  328.9 16.3 %all-gather.19.cloned.1.call-done = bf16[4,256,512]{2,1,0:T(8,128)(2,1)} async-done(((bf16[1,256,512]{2,1,0:T(8,128)(2,1)}), bf16[4,256,512]{2,1,0:T(8,128)(2,1)}) %all-gather.19.cloned.1.call-update) | async-done | bytes 1048592 | tf_op jit(solution)/shard_map/all_gather | solution.py:281
  345.2 1.5 reduce.22
  347.5 38.2 %all-reduce.11.cloned.1.call-done = (bf16[1,128,1536]{2,1,0:T(8,128)(2,1)}, bf16[1,128,512]{2,1,0:T(8,128)(2,1)}) async-done(((bf16[1,128,1536]{2,1,0:T(8,128)(2,1)}, bf16[1,128,512]{2,1,0:T(8,128)(2,1)}), (bf16[1,128,1536]{2,1,0:T(8,128)(2,1)}, bf16[1,128,512]{2,1,0:T(8,128)(2,1)})) %all-reduce.11.cloned.1.call-update) | async-done | bytes 524304 | tf_op jit(solution)/shard_map/psum | solution.py:284
  385.7 1.6 convert_element_type.358
  387.3 2.0 convert_element_type.353
  (262 shorter events, 33.4 us)
Async XLA Ops:
  7.2 90.8 %copy-start = (bf16[1,2,8,16,512]{4,3,2,1,0:T(8,128)(2,1)S(1)}, bf16[1,2,8,16,512]{4,3,2,1,0:T(8,128)(2,1)}, u32[]{:S(2)}) copy-start(bf16[1,2,8,16,512]{4,3,2,1,0:T(8,128)(2,1)} %param.7) | copy-start | bytes 786436
  7.2 64.7 %copy-start.49 = (s32[1,2,8,16]{3,2,1,0:T(8,128)S(1)}, s32[1,2,8,16]{3,2,1,0:T(8,128)}, u32[]{:S(2)}) copy-start(s32[1,2,8,16]{3,2,1,0:T(8,128)} %param.8) | copy-start | bytes 3076
  7.2 70.6 %copy-start.47 = (bf16[1,128,512]{2,1,0:T(8,128)(2,1)S(1)}, bf16[1,128,512]{2,1,0:T(8,128)(2,1)}, u32[]{:S(2)}) copy-start(bf16[1,128,512]{2,1,0:T(8,128)(2,1)} %param.11) | copy-start | bytes 393220
  7.2 31.9 %all-gather.9.cloned.1.call-start = ((), (), s32[]{:S(2)}) async-start(), calls=%async_computation.11 | async-start | bytes 1310720 | tf_op jit(solution)/shard_map/all_gather | solution.py:158
  7.9 80.5 %copy-start.59 = (bf16[1,128]{1,0:T(2,128)(2,1)S(1)}, bf16[1,128]{1,0:T(2,128)(2,1)}, u32[]{:S(2)}) copy-start(bf16[1,128]{1,0:T(2,128)(2,1)} %param.12) | copy-start | bytes 772
  7.9 63.9 %all-gather.13.cloned.1.call-start = ((), (), s32[]{:S(2)}) async-start(), calls=%async_computation.13 | async-start | bytes 1966080 | tf_op jit(solution)/shard_map/all_gather | solution.py:159
  8.7 89.2 %copy-start.42 = (bf16[1,2,8,16,512]{4,3,2,1,0:T(8,128)(2,1)S(1)}, bf16[1,2,8,16,512]{4,3,2,1,0:T(8,128)(2,1)}, u32[]{:S(2)}) copy-start(bf16[1,2,8,16,512]{4,3,2,1,0:T(8,128)(2,1)} %param.13) | copy-start | bytes 786436
  8.7 90.4 %all-gather.11.cloned.1.call-start = ((), (), s32[]{:S(2)}) async-start(), calls=%async_computation.12 | async-start | bytes 3145728 | tf_op jit(solution)/shard_map/all_gather | solution.py:174
  39.1 61.9 %all-gather.15.cloned.1.call-start = ((), (), s32[]{:S(2)}) async-start(), calls=%async_computation.14 | async-start | bytes 4718592 | tf_op jit(solution)/shard_map/all_gather | solution.py:175
  71.8 38.5 %all-gather.17.cloned.1.call-start = ((), (), s32[]{:S(2)}) async-start(), calls=%async_computation.15 | async-start | bytes 1572864 | tf_op jit(solution)/shard_map/all_gather | solution.py:176
  71.9 26.8 %collective-permute-start.3 = (s32[2,4,16]{2,1,0:T(4,128)S(1)}, s32[2,4,16]{2,1,0:T(4,128)S(1)}, u32[]{:S(2)}, u32[]{:S(2)}) collective-permute-start(s32[2,4,16]{2,1,0:T(4,128)S(1)} %get-tuple-element.45), channel_id=1, source_target_pairs={{1,0},{2,1},{3,2},{5,4},{6,5},{7,6},{9,8},{10,9},{11,10},{13,12},{... | collective-permute-start | bytes 1544 | tf_op jit(solution)/shard_map/ppermute | solution.py:23
  73.2 25.5 %collective-permute-start.2 = (s32[2,4,16]{2,1,0:T(4,128)S(1)}, s32[2,4,16]{2,1,0:T(4,128)S(1)}, u32[]{:S(2)}, u32[]{:S(2)}) collective-permute-start(s32[2,4,16]{2,1,0:T(4,128)S(1)} %get-tuple-element.46), channel_id=1, source_target_pairs={{0,1},{1,2},{2,3},{4,5},{5,6},{6,7},{8,9},{9,10},{10,11},{12,13},{... | collective-permute-start | bytes 1544 | tf_op jit(solution)/shard_map/ppermute | solution.py:22
  97.9 4.9 %copy-start.55 = (f32[1,1,512]{2,1,0:T(1,128)}, f32[1,1,512]{2,1,0:T(1,128)S(1)}, u32[]{:S(2)}) copy-start(f32[1,1,512]{2,1,0:T(1,128)S(1)} %get-tuple-element.48) | copy-start | bytes 6148
  98.0 12.4 %copy-start.27 = (bf16[1,1,8,16,512]{4,3,2,1,0:T(8,128)(2,1)}, bf16[1,1,8,16,512]{4,3,2,1,0:T(8,128)(2,1)S(1)}, u32[]{:S(2)}) copy-start(bf16[1,1,8,16,512]{4,3,2,1,0:T(8,128)(2,1)S(1)} %constant_dynamic-slice_fusion) | copy-start | bytes 393220
  99.1 16.0 %copy-start.39 = (pred[128,256]{1,0:T(8,128)(4,1)}, pred[128,256]{1,0:T(8,128)(4,1)S(1)}, u32[]{:S(2)}) copy-start(pred[128,256]{1,0:T(8,128)(4,1)S(1)} %or_and_fusion) | copy-start | bytes 98308
  100.8 16.3 %copy-start.14 = (f32[8,16,512]{2,1,0:T(8,128)}, f32[8,16,512]{2,1,0:T(8,128)S(1)}, u32[]{:S(2)}) copy-start(f32[8,16,512]{2,1,0:T(8,128)S(1)} %get-tuple-element.52) | copy-start | bytes 786436
  101.0 6.6 %copy-start.50 = (f32[8,16]{1,0:T(8,128)}, f32[8,16]{1,0:T(8,128)S(1)}, u32[]{:S(2)}) copy-start(f32[8,16]{1,0:T(8,128)S(1)} %add_rsqrt_fusion.2) | copy-start | bytes 1540
  102.9 9.6 %collective-permute-start = (bf16[4,16,1024]{2,1,0:T(8,128)(2,1)S(1)}, bf16[4,16,1024]{2,1,0:T(8,128)(2,1)S(1)}, u32[]{:S(2)}, u32[]{:S(2)}) collective-permute-start(bf16[4,16,1024]{2,1,0:T(8,128)(2,1)S(1)} %get-tuple-element.34), channel_id=1, source_target_pairs={{0,1},{1,2},{2,3},{4,5},{5,6},{6,7},{8,9},{9,10},{10,11},{12,13},{... | collective-permute-start | bytes 393224 | tf_op jit(solution)/shard_map/ppermute | solution.py:22
  106.3 7.2 %collective-permute-start.1 = (bf16[4,16,1024]{2,1,0:T(8,128)(2,1)S(1)}, bf16[4,16,1024]{2,1,0:T(8,128)(2,1)S(1)}, u32[]{:S(2)}, u32[]{:S(2)}) collective-permute-start(bf16[4,16,1024]{2,1,0:T(8,128)(2,1)S(1)} %get-tuple-element.35), channel_id=1, source_target_pairs={{1,0},{2,1},{3,2},{5,4},{6,5},{7,6},{9,8},{10,9},{11,10},{13,12},{... | collective-permute-start | bytes 393224 | tf_op jit(solution)/shard_map/ppermute | solution.py:23
  116.9 4.6 %copy-start.10 = (bf16[1,128,8,64]{3,2,1,0:T(8,128)(2,1)}, bf16[1,128,8,64]{3,2,1,0:T(8,128)(2,1)S(1)}, u32[]{:S(2)}) copy-start(bf16[1,128,8,64]{3,2,1,0:T(8,128)(2,1)S(1)} %copy.54) | copy-start | bytes 393220
  116.9 4.1 %copy-start.57 = (f32[1,1,512]{2,1,0:T(1,128)S(1)}, f32[1,1,512]{2,1,0:T(1,128)}, u32[]{:S(2)}) copy-start(f32[1,1,512]{2,1,0:T(1,128)} %get-tuple-element.47) | copy-start | bytes 6148
  117.1 3.9 copy-start.60
  123.0 69.7 %all-to-all-start.1 = ((bf16[2,1,8,16,1024]{4,3,2,1,0:T(8,128)(2,1)}), bf16[2,1,8,16,1024]{4,3,2,1,0:T(8,128)(2,1)}, u32[]{:S(2)}, u32[]{:S(2)}) async-start(bf16[2,1,8,16,1024]{4,3,2,1,0:T(8,128)(2,1)} %pad_maximum_fusion.1), calls=%async_computation.1 | async-start | bytes 1048576 | tf_op jit(solution)/shard_map/all_to_all | solution.py:237
  127.3 100.6 %reduce-scatter.7.cloned.1.call-start = ((), (), s32[]{:S(2)}) async-start(), calls=%async_computation.16 | async-start | bytes 1310720 | tf_op jit(solution)/shard_map/reduce_scatter | solution.py:267
  127.7 7.1 %collective-permute-start.4 = (bf16[4,16,1024]{2,1,0:T(8,128)(2,1)}, bf16[4,16,1024]{2,1,0:T(8,128)(2,1)S(1)}, u32[]{:S(2)}, u32[]{:S(2)}) collective-permute-start(bf16[4,16,1024]{2,1,0:T(8,128)(2,1)} %get-tuple-element.32), channel_id=1, source_target_pairs={{0,1},{1,2},{2,3},{4,5},{5,6},{6,7},{8,9},{9,10},{10,11},{12,13},{... | collective-permute-start | bytes 393224 | tf_op jit(solution)/shard_map/ppermute | solution.py:22
  131.1 7.5 %collective-permute-start.5 = (bf16[4,16,1024]{2,1,0:T(8,128)(2,1)S(1)}, bf16[4,16,1024]{2,1,0:T(8,128)(2,1)S(1)}, u32[]{:S(2)}, u32[]{:S(2)}) collective-permute-start(bf16[4,16,1024]{2,1,0:T(8,128)(2,1)S(1)} %get-tuple-element.33), channel_id=1, source_target_pairs={{1,0},{2,1},{3,2},{5,4},{6,5},{7,6},{9,8},{10,9},{11,10},{13,12},{... | collective-permute-start | bytes 393224 | tf_op jit(solution)/shard_map/ppermute | solution.py:23
  133.2 7.1 %copy-start.40 = (pred[128,256]{1,0:T(8,128)(4,1)S(1)}, pred[128,256]{1,0:T(8,128)(4,1)}, u32[]{:S(2)}) copy-start(pred[128,256]{1,0:T(8,128)(4,1)} %copy-done.39) | copy-start | bytes 98308
  139.4 5.1 %copy-start.2 = (bf16[1,128,2,8,64]{1,4,3,2,0:T(8,128)(2,1)}, bf16[1,128,2,8,64]{1,4,3,2,0:T(8,128)(2,1)S(1)}, u32[]{:S(2)}) copy-start(bf16[1,128,2,8,64]{1,4,3,2,0:T(8,128)(2,1)S(1)} %copy.55) | copy-start | bytes 786436
  140.3 4.3 %copy-start.4 = (bf16[1,128,2,8,64]{1,4,3,2,0:T(8,128)(2,1)}, bf16[1,128,2,8,64]{1,4,3,2,0:T(8,128)(2,1)S(1)}, u32[]{:S(2)}) copy-start(bf16[1,128,2,8,64]{1,4,3,2,0:T(8,128)(2,1)S(1)} %copy.56) | copy-start | bytes 786436
  144.5 3.9 copy-start.46
  152.7 10.8 %copy-start.13 = (f32[8,16,512]{2,1,0:T(8,128)S(1)}, f32[8,16,512]{2,1,0:T(8,128)}, u32[]{:S(2)}) copy-start(f32[8,16,512]{2,1,0:T(8,128)} %copy-done.12) | copy-start | bytes 786436
  152.7 10.8 %copy-start.20 = (bf16[8,16,512]{2,1,0:T(8,128)(2,1)S(1)}, bf16[8,16,512]{2,1,0:T(8,128)(2,1)}, u32[]{:S(2)}) copy-start(bf16[8,16,512]{2,1,0:T(8,128)(2,1)} %reshape.698) | copy-start | bytes 393220
  152.7 10.8 %copy-start.53 = (f32[8,16]{1,0:T(8,128)S(1)}, f32[8,16]{1,0:T(8,128)}, u32[]{:S(2)}) copy-start(f32[8,16]{1,0:T(8,128)} %copy-done.52) | copy-start | bytes 1540
  152.7 10.8 %copy-start.58 = (f32[1,1,512]{2,1,0:T(1,128)S(1)}, f32[1,1,512]{2,1,0:T(1,128)}, u32[]{:S(2)}) copy-start(f32[1,1,512]{2,1,0:T(1,128)} %get-tuple-element.47) | copy-start | bytes 6148
  153.7 5.3 %collective-permute-start.6 = (bf16[4,16,1024]{2,1,0:T(8,128)(2,1)S(1)}, bf16[4,16,1024]{2,1,0:T(8,128)(2,1)S(1)}, u32[]{:S(2)}, u32[]{:S(2)}) collective-permute-start(bf16[4,16,1024]{2,1,0:T(8,128)(2,1)S(1)} %get-tuple-element.28), channel_id=1, source_target_pairs={{0,1},{1,2},{2,3},{4,5},{5,6},{6,7},{8,9},{9,10},{10,11},{12,13},{... | collective-permute-start | bytes 393224 | tf_op jit(solution)/shard_map/ppermute | solution.py:22
  156.5 6.9 %collective-permute-start.7 = (bf16[4,16,1024]{2,1,0:T(8,128)(2,1)S(1)}, bf16[4,16,1024]{2,1,0:T(8,128)(2,1)S(1)}, u32[]{:S(2)}, u32[]{:S(2)}) collective-permute-start(bf16[4,16,1024]{2,1,0:T(8,128)(2,1)S(1)} %get-tuple-element.29), channel_id=1, source_target_pairs={{1,0},{2,1},{3,2},{5,4},{6,5},{7,6},{9,8},{10,9},{11,10},{13,12},{... | collective-permute-start | bytes 393224 | tf_op jit(solution)/shard_map/ppermute | solution.py:23
  159.0 6.8 %copy-start.43 = (bf16[1,2,8,16,512]{4,3,2,1,0:T(8,128)(2,1)S(1)}, bf16[1,2,8,16,512]{4,3,2,1,0:T(8,128)(2,1)}, u32[]{:S(2)}) copy-start(bf16[1,2,8,16,512]{4,3,2,1,0:T(8,128)(2,1)} %param.13) | copy-start | bytes 786436
  163.4 3.2 copy-start.31
  163.4 3.2 copy-start.33
  166.7 4.5 %copy-start.7 = (bf16[1,128,2,8,64]{1,4,3,2,0:T(8,128)(2,1)S(1)}, bf16[1,128,2,8,64]{1,4,3,2,0:T(8,128)(2,1)}, u32[]{:S(2)}) copy-start(bf16[1,128,2,8,64]{1,4,3,2,0:T(8,128)(2,1)} %copy-done.6) | copy-start | bytes 786436
  166.7 4.5 %copy-start.9 = (bf16[1,128,2,8,64]{1,4,3,2,0:T(8,128)(2,1)S(1)}, bf16[1,128,2,8,64]{1,4,3,2,0:T(8,128)(2,1)}, u32[]{:S(2)}) copy-start(bf16[1,128,2,8,64]{1,4,3,2,0:T(8,128)(2,1)} %copy-done.8) | copy-start | bytes 786436
  166.7 4.5 %copy-start.54 = (f32[8,128]{1,0:T(8,128)S(1)}, f32[8,128]{1,0:T(8,128)}, u32[]{:S(2)}) copy-start(f32[8,128]{1,0:T(8,128)} %multiply_divide_fusion) | copy-start | bytes 12292
  179.0 11.1 %copy-start.15 = (f32[8,16,512]{2,1,0:T(8,128)S(1)}, f32[8,16,512]{2,1,0:T(8,128)}, u32[]{:S(2)}) copy-start(f32[8,16,512]{2,1,0:T(8,128)} %copy-done.14) | copy-start | bytes 786436
  179.0 11.1 %copy-start.25 = (bf16[8,16,512]{2,1,0:T(8,128)(2,1)S(1)}, bf16[8,16,512]{2,1,0:T(8,128)(2,1)}, u32[]{:S(2)}) copy-start(bf16[8,16,512]{2,1,0:T(8,128)(2,1)} %reshape.702) | copy-start | bytes 393220
  179.1 11.1 %copy-start.51 = (f32[8,16]{1,0:T(8,128)S(1)}, f32[8,16]{1,0:T(8,128)}, u32[]{:S(2)}) copy-start(f32[8,16]{1,0:T(8,128)} %copy-done.50) | copy-start | bytes 1540
  179.1 11.1 %copy-start.56 = (f32[1,1,512]{2,1,0:T(1,128)S(1)}, f32[1,1,512]{2,1,0:T(1,128)}, u32[]{:S(2)}) copy-start(f32[1,1,512]{2,1,0:T(1,128)} %copy-done.55) | copy-start | bytes 6148
  179.8 5.9 %collective-permute-start.8 = (bf16[4,16,1024]{2,1,0:T(8,128)(2,1)S(1)}, bf16[4,16,1024]{2,1,0:T(8,128)(2,1)S(1)}, u32[]{:S(2)}, u32[]{:S(2)}) collective-permute-start(bf16[4,16,1024]{2,1,0:T(8,128)(2,1)S(1)} %get-tuple-element.22), channel_id=1, source_target_pairs={{0,1},{1,2},{2,3},{4,5},{5,6},{6,7},{8,9},{9,10},{10,11},{12,13},{... | collective-permute-start | bytes 393224 | tf_op jit(solution)/shard_map/ppermute | solution.py:22
  183.2 6.9 %collective-permute-start.9 = (bf16[4,16,1024]{2,1,0:T(8,128)(2,1)S(1)}, bf16[4,16,1024]{2,1,0:T(8,128)(2,1)S(1)}, u32[]{:S(2)}, u32[]{:S(2)}) collective-permute-start(bf16[4,16,1024]{2,1,0:T(8,128)(2,1)S(1)} %get-tuple-element.23), channel_id=1, source_target_pairs={{1,0},{2,1},{3,2},{5,4},{6,5},{7,6},{9,8},{10,9},{11,10},{13,12},{... | collective-permute-start | bytes 393224 | tf_op jit(solution)/shard_map/ppermute | solution.py:23
  184.6 7.9 %copy-start.45 = (bf16[8,16,1024]{2,1,0:T(8,128)(2,1)S(1)}, bf16[8,16,1024]{2,1,0:T(8,128)(2,1)}, u32[]{:S(2)}) copy-start(bf16[8,16,1024]{2,1,0:T(8,128)(2,1)} %copy-done.44) | copy-start | bytes 786436
  199.2 5.2 %copy-start.21 = (bf16[8,16,512]{2,1,0:T(8,128)(2,1)S(1)}, bf16[8,16,512]{2,1,0:T(8,128)(2,1)}, u32[]{:S(2)}) copy-start(bf16[8,16,512]{2,1,0:T(8,128)(2,1)} %reshape.698) | copy-start | bytes 393220
  199.2 5.3 %copy-start.32 = (bf16[4,16,1024]{2,1,0:T(8,128)(2,1)S(1)}, bf16[4,16,1024]{2,1,0:T(8,128)(2,1)}, u32[]{:S(2)}) copy-start(bf16[4,16,1024]{2,1,0:T(8,128)(2,1)} %copy-done.31) | copy-start | bytes 393220
  199.2 5.3 %copy-start.34 = (bf16[4,16,1024]{2,1,0:T(8,128)(2,1)S(1)}, bf16[4,16,1024]{2,1,0:T(8,128)(2,1)}, u32[]{:S(2)}) copy-start(bf16[4,16,1024]{2,1,0:T(8,128)(2,1)} %copy-done.33) | copy-start | bytes 393220
  199.3 5.3 %copy-start.28 = (bf16[1,1,8,16,512]{4,3,2,1,0:T(8,128)(2,1)S(1)}, bf16[1,1,8,16,512]{4,3,2,1,0:T(8,128)(2,1)}, u32[]{:S(2)}) copy-start(bf16[1,1,8,16,512]{4,3,2,1,0:T(8,128)(2,1)} %copy-done.27) | copy-start | bytes 393220
  199.5 5.1 %copy-start.26 = (bf16[8,16,512]{2,1,0:T(8,128)(2,1)S(1)}, bf16[8,16,512]{2,1,0:T(8,128)(2,1)}, u32[]{:S(2)}) copy-start(bf16[8,16,512]{2,1,0:T(8,128)(2,1)} %reshape.702) | copy-start | bytes 393220
  199.5 5.1 %copy-start.36 = (bf16[4,16,1024]{2,1,0:T(8,128)(2,1)S(1)}, bf16[4,16,1024]{2,1,0:T(8,128)(2,1)}, u32[]{:S(2)}) copy-start(bf16[4,16,1024]{2,1,0:T(8,128)(2,1)} %copy-done.35) | copy-start | bytes 393220
  199.5 5.1 %copy-start.38 = (bf16[4,16,1024]{2,1,0:T(8,128)(2,1)S(1)}, bf16[4,16,1024]{2,1,0:T(8,128)(2,1)}, u32[]{:S(2)}) copy-start(bf16[4,16,1024]{2,1,0:T(8,128)(2,1)} %copy-done.37) | copy-start | bytes 393220
  201.0 5.0 %all-to-all-start.5 = ((bf16[2,1,8,16,512]{4,3,2,1,0:T(8,128)(2,1)}), bf16[2,1,8,16,512]{4,3,2,1,0:T(8,128)(2,1)S(1)}, u32[]{:S(2)}, u32[]{:S(2)}) async-start(bf16[2,1,8,16,512]{4,3,2,1,0:T(8,128)(2,1)} %pad_maximum_fusion.13), calls=%async_computation.7 | async-start | bytes 524288 | tf_op jit(solution)/shard_map/all_to_all | solution.py:241
  204.4 49.6 %reduce-scatter.11.cloned.1.call-start = ((), (), s32[]{:S(2)}) async-start(), calls=%async_computation.18 | async-start | bytes 655360 | tf_op jit(solution)/shard_map/reduce_scatter | solution.py:273
  211.8 5.0 %all-to-all-start.3 = ((bf16[2,1,8,16,512]{4,3,2,1,0:T(8,128)(2,1)}), bf16[2,1,8,16,512]{4,3,2,1,0:T(8,128)(2,1)S(1)}, u32[]{:S(2)}, u32[]{:S(2)}) async-start(bf16[2,1,8,16,512]{4,3,2,1,0:T(8,128)(2,1)} %pad_maximum_fusion.12), calls=%async_computation.4 | async-start | bytes 524288 | tf_op jit(solution)/shard_map/all_to_all | solution.py:239
  215.2 73.0 %reduce-scatter.9.cloned.1.call-start = ((), (), s32[]{:S(2)}) async-start(), calls=%async_computation.17 | async-start | bytes 1966080 | tf_op jit(solution)/shard_map/reduce_scatter | solution.py:270
  222.9 92.8 %reduce-scatter.13.cloned.1.call-start = ((), (), s32[]{:S(2)}) async-start(), calls=%async_computation.20 | async-start | bytes 163840
  224.8 63.6 %copy-start.17 = (bf16[2,512,512]{2,1,0:T(8,128)(2,1)S(1)}, bf16[2,512,512]{2,1,0:T(8,128)(2,1)}, u32[]{:S(2)}) copy-start(bf16[2,512,512]{2,1,0:T(8,128)(2,1)} %all-gather.17.cloned.1.call-done) | copy-start | bytes 3145732
  227.8 117.4 %all-gather.19.cloned.1.call-start = ((), (), s32[]{:S(2)}) async-start(), calls=%async_computation.19 | async-start | bytes 1310720 | tf_op jit(solution)/shard_map/all_gather | solution.py:281
  228.4 157.3 %all-reduce.11.cloned.1.call-start = ((), (), s32[]{:S(2)}) async-start(), calls=%async_computation.21 | async-start | bytes 1048576 | tf_op jit(solution)/shard_map/psum | solution.py:284
  (22 other events, 44.6 us)
Sparse Core Ops, SparseCore 0:
  9.9 29.2 all-gather.8
  40.9 30.8 all-gather.12
  73.4 10.5 all-gather.10
  85.4 13.2 all-gather.14
  100.1 10.1 all-gather.16
  199.4 26.0 reduce-scatter.6
  228.9 25.1 reduce-scatter.10
  257.0 31.1 reduce-scatter.8
  291.5 24.1 reduce-scatter.12
  317.1 27.9 all-gather.18
  347.6 38.0 all-reduce.10
